TPU v7x, 32 devices: a whole 2x2x4 slice. The times are simulated.
32 devices in a mesh: tm: 8 (over z, core), mp: 2 (over y), batch: 2 (over x).
Axes of the slice: x: 2, y: 2, z: 4, core: 2. Of those that a mesh axis runs over, the one named last changes fastest.
Arguments:
- frames: bfloat16 [16384, 1024], P(('batch', 'tm')), parts along dimension 0, may hold values from -40 to 40
- norm_gain: float32 [1024], replicated, may hold values from 0.5 to 1.5
- qkv_weight: bfloat16 [3, 1024, 1024], P(None, None, 'mp'), may hold values from -2 to 2
- out_weight: bfloat16 [1024, 1024], P('mp'), may hold values from -0.1875 to 0.1875
- cotangent: bfloat16 [16384, 1024], P(('batch', 'tm')), parts along dimension 0, may hold values from -6 to 6
- pad_mask: int32 [16384], P('batch'), parts along dimension 0, may hold values from 0 to 1, as said below
- utt_lengths: int32 [16], P('batch'), parts along dimension 0, may hold values from 1 to 2048, 8192 in all
Outputs:
- frame_grad: bfloat16 [16384, 1024], P(('batch', 'tm'), 'mp'), parts along dimension 0
- qkv_grad: float32 [6, 1024, 1024], P('batch', 'tm', 'mp'), parts along dimension 0
- out_grad: float32 [2048, 1024], P(('batch', 'mp'), 'tm'), parts along dimension 0
There are 2 independent parts, one for each index of `batch`. A program takes and returns all parts, laid end to end along the dimension named above; an argument that names none is the same for every part. Nothing has to cross between parts.
Inputs may be any that keep to these rules, and one draw needn't show every extreme that they name: `pad_mask`: in each aligned block of 256 frames, the padding frames form the tail of the block, fewer than 128 of them. `utt_lengths`: 8 lengths that sum to 8192; the largest is exactly 2048.
All inputs are finite; a program needn't handle non-finite values.
Results may differ from a plain program's by a relative error of at most 0.012.
The roundings to bfloat16 on the way count: a program that leaves them out, or rounds other values in their place, can miss the bound.
Values may be sent and summed in bfloat16 or wider, within the bound.
A program may use at most 128 MiB of HBM per device.

v0:
```python
import jax
import jax.numpy as jnp
from jax import lax
from jax.sharding import PartitionSpec as P

HS = 128
CH = 32
EPSILON = 1e-05


def with_halo(block, sides, width):
    for axis, dim in sides:
        count = lax.axis_size(axis)
        forward = [(i, i + 1) for i in range(count - 1)]
        backward = [(target, source) for source, target in forward]
        low = lax.ppermute(
            lax.slice_in_dim(block, block.shape[dim] - width, None, axis=dim), axis, forward
        )
        high = lax.ppermute(lax.slice_in_dim(block, 0, width, axis=dim), axis, backward)
        block = jnp.concatenate([low, block, high], axis=dim)
    return block


def layer_norm(frames, norm_gain):
    values = frames.astype(jnp.float32)
    center = values - jnp.mean(values, axis=-1, keepdims=True)
    inverse = lax.rsqrt(jnp.mean(center * center, axis=-1, keepdims=True) + EPSILON)
    normal_form = center * inverse
    return (normal_form, inverse, (normal_form * norm_gain).astype(jnp.bfloat16))


def norm_backward(incoming, normal_form, inverse, norm_gain):
    scaled = incoming * norm_gain
    mean_grad = jnp.mean(scaled, axis=-1, keepdims=True)
    mean_proj = jnp.mean(scaled * normal_form, axis=-1, keepdims=True)
    return inverse * (scaled - mean_grad - normal_form * mean_proj)


def windows(block_rows):
    block_count = block_rows.shape[0] - 2
    return jnp.concatenate(
        [block_rows[:block_count], block_rows[1 : block_count + 1], block_rows[2:]], axis=1
    )


def fold_keys(window):
    block_width = window.shape[1] // 3
    trailing = [(0, 0)] * (window.ndim - 1)
    pieces = [
        jnp.pad(
            window[:, offset * block_width : (offset + 1) * block_width],
            [(offset, 2 - offset)] + trailing,
        )
        for offset in range(3)
    ]
    return pieces[0] + pieces[1] + pieces[2]


def permitted(query_start, query_count, key_start, key_count, pad_mask, utt_lengths):
    utt_ends = jnp.cumsum(utt_lengths)
    query_pos = query_start + jnp.arange(query_count, dtype=jnp.int32)
    key_pos = key_start + jnp.arange(key_count, dtype=jnp.int32)

    def segment(positions):
        return jnp.sum((utt_ends[None, :] <= positions[:, None]).astype(jnp.int32), axis=1)

    padded = jnp.pad(pad_mask, 2 * CH)
    live_keys = lax.dynamic_slice(
        padded, (jnp.asarray(key_start + 2 * CH, jnp.int32),), (key_count,)
    )
    query_cells = query_pos.reshape(-1, CH)
    query_seg = segment(query_pos).reshape(-1, CH)
    key_cells = windows(key_pos.reshape(-1, CH))
    key_seg = windows(segment(key_pos).reshape(-1, CH))
    key_live = windows(live_keys.reshape(-1, CH))
    same_utt = query_seg[:, :, None] == key_seg[:, None, :]
    return same_utt & (
        (key_live[:, None, :] == 1) | (query_cells[:, :, None] == key_cells[:, None, :])
    )


def attend(queries, grad_rows, key_blocks, value_blocks, allowed):
    score_scale = HS ** (-0.5)
    key_win = windows(key_blocks)
    value_win = windows(value_blocks)
    scores = (
        jnp.einsum("cihd,cjhd->chij", queries, key_win, preferred_element_type=jnp.float32)
        * score_scale
    )
    scores = jnp.where(allowed[:, None], scores, -1e30)
    row_max = jnp.max(scores, axis=-1, keepdims=True)
    weights = jnp.exp(scores - row_max)
    attn_probs = weights / jnp.sum(weights, axis=-1, keepdims=True)
    rounded = attn_probs.astype(jnp.bfloat16)
    mixed_out = jnp.einsum(
        "chij,cjhd->cihd", rounded, value_win, preferred_element_type=jnp.float32
    ).astype(jnp.bfloat16)
    prob_grad = jnp.einsum(
        "cihd,cjhd->chij", grad_rows, value_win, preferred_element_type=jnp.float32
    )
    centre = jnp.sum(attn_probs * prob_grad, axis=-1, keepdims=True)
    score_grad = (attn_probs * (prob_grad - centre) * score_scale).astype(jnp.bfloat16)
    query_grad = jnp.einsum(
        "chij,cjhd->cihd", score_grad, key_win, preferred_element_type=jnp.float32
    )
    key_grad = fold_keys(
        jnp.einsum("chij,cihd->cjhd", score_grad, queries, preferred_element_type=jnp.float32)
    )
    value_grad = fold_keys(
        jnp.einsum("chij,cihd->cjhd", rounded, grad_rows, preferred_element_type=jnp.float32)
    )
    return (mixed_out, query_grad, key_grad, value_grad)


def on_device(frames, norm_gain, qkv_weight, out_weight, cotangent, pad_mask, utt_lengths):
    frame_rows = frames.shape[0]
    head_cols = qkv_weight.shape[2]
    heads_here = head_cols // HS
    first_row = lax.axis_index("tm") * frame_rows
    normal_form, inverse, normed = layer_norm(frames, norm_gain)
    projected = jnp.einsum(
        "rd,mdh->mrh", normed, qkv_weight, preferred_element_type=jnp.float32
    ).astype(jnp.bfloat16)
    live_rows = lax.dynamic_slice(pad_mask, (first_row,), (frame_rows,))
    masked = cotangent * live_rows.astype(jnp.bfloat16)[:, None]
    grad_heads = jnp.dot(masked, out_weight.T, preferred_element_type=jnp.float32).astype(
        jnp.bfloat16
    )

    def blocks(tensor):
        return tensor.reshape(-1, CH, heads_here, HS)

    stacked = jnp.concatenate([projected, grad_heads[None]], axis=0)
    extended = with_halo(stacked, (("tm", 1),), 2 * CH)
    query_rim = extended[:, CH:-CH]
    allowed = permitted(
        first_row - CH,
        frame_rows + 2 * CH,
        first_row - 2 * CH,
        frame_rows + 4 * CH,
        pad_mask,
        utt_lengths,
    )
    mixed_ext, query_ext, key_ext, value_ext = attend(
        blocks(query_rim[0]),
        blocks(query_rim[3]),
        blocks(extended[1]),
        blocks(extended[2]),
        allowed,
    )
    mixed_out = mixed_ext[1:-1]
    query_grad = query_ext[1:-1]
    key_grad = key_ext[2:-2]
    value_grad = value_ext[2:-2]
    all_grads = (
        jnp.stack([query_grad, key_grad, value_grad])
        .reshape(3, frame_rows, head_cols)
        .astype(jnp.bfloat16)
    )
    mixed_rows = mixed_out.reshape(frame_rows, head_cols)
    weight_terms = jnp.einsum("rd,mrh->mdh", normed, all_grads, preferred_element_type=jnp.float32)
    out_terms = jnp.einsum("rh,rd->hd", mixed_rows, masked, preferred_element_type=jnp.float32)
    qkv_grad, out_grad = (
        lax.psum_scatter(weight_terms, "tm", scatter_dimension=1, tiled=True),
        lax.psum_scatter(out_terms, "tm", scatter_dimension=1, tiled=True),
    )
    incoming = jnp.einsum("mrh,mdh->rd", all_grads, qkv_weight, preferred_element_type=jnp.float32)
    head_total = lax.psum(incoming, "mp")
    full_grad = norm_backward(head_total, normal_form, inverse, norm_gain)
    share_cols = full_grad.shape[1] // lax.axis_size("mp")
    frame_grad = lax.dynamic_slice_in_dim(
        full_grad, lax.axis_index("mp") * share_cols, share_cols, 1
    )
    return (frame_grad.astype(jnp.bfloat16), qkv_grad, out_grad)


def solution(mesh):
    placed = (
        P(("batch", "tm"), None),
        P(),
        P(None, None, "mp"),
        P("mp", None),
        P(("batch", "tm"), None),
        P("batch"),
        P("batch"),
    )
    return jax.shard_map(
        on_device,
        mesh=mesh,
        in_specs=placed,
        out_specs=(P(("batch", "tm"), "mp"), P("batch", "tm", "mp"), P(("batch", "mp"), "tm")),
        check_vma=False,
    )
```

profile of v0, /device:TPU:0, one launch (start us, length us, event | category | flops | bytes accessed | tf_op | source)
XLA Modules:
  0.0 311.9 jit_solution(12134649921171048453)
XLA Ops:
  11.2 3.3 %fusion.34 = bf16[1,1024,512]{2,1,0:T(8,128)(2,1)S(1)} fusion(bf16[512,1024]{1,0:T(8,128)(2,1)} %param.10, bf16[1024,1024]{1,0:T(8,128)(2,1)} %param.11, bf16[1024]{0:T(1024)(128)(2,1)S(1)} %dynamic-slice_convert_fusion), kind=kOutput, calls=%fused_computation.43 | convolution fusion | flops 1075314688 | bytes 4196352 | tf_op jit(solution)/shard_map/dot_general | solution.py:126
  14.6 4.0 %convert_bitcast_fusion = bf16[3,1024,512]{2,1,0:T(8,128)(2,1)S(1)} fusion(bf16[3,1024,512]{2,1,0:T(8,128)(2,1)S(1)} %copy-done, f32[1024]{0:T(1024)S(1)} %copy-done.22, bf16[1024,1024]{1,0:T(8,128)(2,1)S(1)} %copy-done.3, f32[1024]{0:T(1024)S(1)} %add_rsqrt_fusion, f32[1024]{0:T(1024)S(1)} %broadcast_multiply_fusion.3), kind=kOutput, calls=%fused_computation.9 | convolution fusion | flops 3228041216 | bytes 8400896 | tf_op jit(solution)/shard_map/rd,mdh->mrh/dot_general | solution.py:121
  21.7 3.7 %collective-permute-start = (bf16[4,64,512]{2,1,0:T(8,128)(2,1)}, bf16[4,64,512]{2,1,0:T(8,128)(2,1)}, u32[]{:S(2)}, u32[]{:S(2)}) collective-permute-start(bf16[4,64,512]{2,1,0:T(8,128)(2,1)} %get-tuple-element.30), channel_id=1, source_target_pairs={{0,4},{4,8},{8,12},{12,16},{16,20},{20,24},{24,28},{1,5},{5,9},{9,... | collective-permute-start | bytes 786440 | tf_op jit(solution)/shard_map/ppermute | solution.py:16
  33.4 3.2 %pad_maximum_fusion = (bf16[1,1088,512]{2,1,0:T(8,128)(2,1)}, bf16[1,1088,512]{2,1,0:T(8,128)(2,1)}, bf16[1,1088,512]{2,1,0:T(8,128)(2,1)}) fusion(bf16[4,64,512]{2,1,0:T(8,128)(2,1)S(1)} %collective-permute-done.1, bf16[1,1024,512]{2,1,0:T(8,128)(2,1)} %copy-done.4, bf16[3,1024,512]{2,1,0:T(8,128)(2,1)} %copy-done.1, ...), kind=kLoop, calls=%fused_computation.44 | loop fusion | flops 10027008 | bytes 8060928 | tf_op jit(solution)/shard_map/concatenate | solution.py:20
  36.7 3.1 slice.216
  39.8 4.2 %pad_maximum_fusion.11 = (bf16[1,1088,512]{2,1,0:T(8,128)(2,1)}, bf16[1,1088,512]{2,1,0:T(8,128)(2,1)}, bf16[1,1088,512]{2,1,0:T(8,128)(2,1)}, bf16[1,1088,512]{2,1,0:T(8,128)(2,1)}, bf16[1,1088,512]{2,1,0:T(8,128)(2,1)}) fusion(bf16[4,64,512]{2,1,0:T(8,128)(2,1)S(1)} %collective-permute-done.1, bf16[4,64,512]{2,1,0:T(8,128)(2,1)} %collective-permute-done, ...), kind=kLoop, calls=%fused_computation.55 | loop fusion | flops 21168128 | bytes 10289152 | tf_op jit(solution)/shard_map/slice | solution.py:145
  44.0 3.1 reshape_squeeze.8
  47.1 3.1 reshape_squeeze.9
  50.2 3.1 slice.194
  53.3 3.1 slice.214
  56.4 3.1 slice.191
  59.4 3.1 slice.196
  62.5 3.1 slice.212
  69.0 3.2 %fusion.47 = f32[34,4,32,96]{3,2,1,0:T(8,128)} fusion(bf16[34,96,4,128]{3,1,2,0:T(8,128)(2,1)S(1)} %copy_dynamic-update-slice_fusion, bf16[34,32,4,128]{3,2,1,0:T(4,128)(2,1)S(1)} %copy-done.8), kind=kOutput, calls=%fused_computation.73 | convolution fusion | flops 106954752 | bytes 6127616 | tf_op jit(solution)/shard_map/cihd,cjhd->chij/dot_general | solution.py:98
  77.8 28.3 %fusion.31 = bf16[34,32,4,128]{3,1,2,0:T(8,128)(2,1)} fusion(bf16[34,96,4,128]{3,1,2,0:T(8,128)(2,1)} %copy-done.6, f32[34,4,32,96]{3,2,1,0:T(8,128)} %fusion.47, f32[34,4,32,96]{3,2,1,0:T(8,128)} %get-tuple-element.42, f32[34,4,32]{2,1,0:T(4,128)S(1)} %get-tuple-element.41), kind=kOutput, calls=%fused_computation.42 | convolution fusion | flops 110440800 | bytes 7816192 | tf_op jit(solution)/shard_map/chij,cjhd->cihd/dot_general | solution.py:103
  106.1 31.5 %convolution_bitcast_fusion.1 = f32[34,96,4,128]{3,1,2,0:T(8,128)} fusion(f32[34,4,32,96]{3,2,1,0:T(8,128)} %fusion.47, bf16[34,32,4,128]{3,2,1,0:T(4,128)(2,1)} %reshape_squeeze.8, f32[34,4,32,96]{3,2,1,0:T(8,128)} %get-tuple-element.42, f32[34,4,32]{2,1,0:T(4,128)S(1)} %get-tuple-element.41), kind=kOutput, calls=%fused_computation.11 | convolution fusion | flops 109883744 | bytes 11158528 | tf_op jit(solution)/shard_map/chij,cihd->cjhd/dot_general | solution.py:107
  137.6 13.4 %convolution_bitcast_fusion = f32[34,96,4,128]{3,1,2,0:T(8,128)} fusion(bf16[34,32,4,128]{3,2,1,0:T(4,128)(2,1)} %reshape_squeeze.9, f32[34,4,32]{2,1,0:T(4,128)S(1)} %get-tuple-element.41, f32[34,4,32,96]{3,2,1,0:T(8,128)} %copy-done.5, pred[34,32,96]{2,1,0:T(8,128)(4,1)S(1)} %or_and_fusion), kind=kOutput, calls=%fused_computation.10 | convolution fusion | flops 109048160 | bytes 9591808 | tf_op jit(solution)/shard_map/chij,cihd->cjhd/dot_general | solution.py:110
  156.0 3.8 %fusion.66 = (f32[34,32,4,128]{3,1,2,0:T(8,128)S(1)}, f32[34,32,4,128]{3,1,2,0:T(8,128)S(1)}, f32[34,32,4,128]{3,1,2,0:T(8,128)S(1)}) fusion(f32[34,96,4,128]{3,1,2,0:T(8,128)} %convolution_bitcast_fusion.1), kind=kLoop, calls=%fused_computation.111 | loop fusion | bytes 13369344 | tf_op jit(solution)/shard_map/slice | solution.py:51
  166.6 3.8 %fusion.65 = (f32[34,32,4,128]{3,1,2,0:T(8,128)S(1)}, f32[34,32,4,128]{3,1,2,0:T(8,128)S(1)}, f32[34,32,4,128]{3,1,2,0:T(8,128)S(1)}) fusion(f32[34,96,4,128]{3,1,2,0:T(8,128)} %convolution_bitcast_fusion), kind=kLoop, calls=%fused_computation.110 | loop fusion | bytes 13369344 | tf_op jit(solution)/shard_map/slice | solution.py:51
  178.6 6.9 %convolution_bitcast_fusion.3 = f32[1024,1024]{1,0:T(8,128)} fusion(bf16[3,1024,512]{2,1,0:T(8,128)(2,1)} %constant_dynamic-update-slice_fusion, bf16[3,1024,512]{2,1,0:T(8,128)(2,1)S(1)} %copy-done), kind=kOutput, calls=%fused_computation.18 | convolution fusion | flops 3221225472 | bytes 10485760 | tf_op jit(solution)/shard_map/mrh,mdh->rd/dot_general | solution.py:167
  186.2 8.8 %convolution_bitcast_fusion.2 = f32[3,1024,512]{1,2,0:T(8,128)} fusion(bf16[3,1024,512]{2,1,0:T(8,128)(2,1)} %constant_dynamic-update-slice_fusion, f32[1024]{0:T(1024)S(1)} %copy-done.23, bf16[1024,1024]{1,0:T(8,128)(2,1)} %param.7, f32[1024]{0:T(1024)S(1)} %add_rsqrt_fusion, f32[1024]{0:T(1024)S(1)} %copy-done.19), kind=kOutput, calls=%fused_computation.12 | convolution fusion | flops 3226468352 | bytes 11546624 | tf_op jit(solution)/shard_map/rd,mrh->mdh/dot_general | solution.py:161
  195.1 11.3 %fusion.30 = bf16[34,32,4,128]{3,1,2,0:T(8,128)(2,1)} fusion(bf16[34,96,4,128]{3,1,2,0:T(8,128)(2,1)} %copy-done.7, f32[34,4,32]{2,1,0:T(4,128)S(1)} %get-tuple-element.41, f32[34,4,32,96]{3,2,1,0:T(8,128)} %copy-done.5, pred[34,32,96]{2,1,0:T(8,128)(4,1)S(1)} %or_and_fusion), kind=kOutput, calls=%fused_computation.41 | convolution fusion | flops 109605216 | bytes 6249472 | tf_op jit(solution)/shard_map/chij,cjhd->cihd/dot_general | solution.py:95
  211.1 84.6 %all-reduce.9.cloned.1.call-done = f32[1024,1024]{1,0:T(8,128)} async-done(((f32[1024,1024]{1,0:T(8,128)}), f32[1024,1024]{1,0:T(8,128)}) %all-reduce.9.cloned.1.call-update) | async-done | bytes 4194320 | tf_op jit(solution)/shard_map/psum | solution.py:168
  295.6 3.9 %fusion.64 = (f32[1024]{0:T(1024)S(1)}, f32[1024]{0:T(1024)S(1)}, f32[1024,1024]{1,0:T(8,128)S(1)}, f32[1024,1024]{1,0:T(8,128)S(1)}) fusion(f32[1024]{0:T(1024)S(1)} %add_rsqrt_fusion, f32[1024]{0:T(1024)S(1)} %copy-done.19, bf16[1024,1024]{1,0:T(8,128)(2,1)} %param.7, f32[1024,1024]{1,0:T(8,128)} %all-reduce.9.cloned.1.call-done, f32[1024]{0:T(1024)S(1)} %copy-done.23), kind=kLoop, calls=%fused_computation.109 | loop fusion | flops 7337984 | bytes 14700544 | tf_op jit(solution)/shard_map/reduce_sum | solution.py:34
  (116 shorter events, 53.1 us)
Async XLA Ops:
  8.0 6.5 %copy-start = (bf16[3,1024,512]{2,1,0:T(8,128)(2,1)S(1)}, bf16[3,1024,512]{2,1,0:T(8,128)(2,1)}, u32[]{:S(2)}) copy-start(bf16[3,1024,512]{2,1,0:T(8,128)(2,1)} %param.9) | copy-start | bytes 9437188
  8.0 287.6 %all-reduce.9.cloned.1.call-start = ((), (), s32[]{:S(2)}) async-start(), calls=%async_computation.2 | async-start | bytes 8388608 | tf_op jit(solution)/shard_map/psum | solution.py:168
  8.1 2.4 copy-start.2
  8.1 3.1 copy-start.17
  10.4 4.1 %copy-start.18 = (f32[1024]{0:T(1024)}, f32[1024]{0:T(1024)S(1)}, u32[]{:S(2)}) copy-start(f32[1024]{0:T(1024)S(1)} %broadcast_multiply_fusion.3) | copy-start | bytes 12292
  11.2 3.4 %copy-start.20 = (bf16[1024]{0:T(1024)(128)(2,1)}, bf16[1024]{0:T(1024)(128)(2,1)S(1)}, u32[]{:S(2)}) copy-start(bf16[1024]{0:T(1024)(128)(2,1)S(1)} %dynamic-slice_convert_fusion) | copy-start | bytes 6148
  11.2 3.4 %copy-start.3 = (bf16[1024,1024]{1,0:T(8,128)(2,1)S(1)}, bf16[1024,1024]{1,0:T(8,128)(2,1)}, u32[]{:S(2)}) copy-start(bf16[1024,1024]{1,0:T(8,128)(2,1)} %param.7) | copy-start | bytes 6291460
  11.2 3.4 %copy-start.22 = (f32[1024]{0:T(1024)S(1)}, f32[1024]{0:T(1024)}, u32[]{:S(2)}) copy-start(f32[1024]{0:T(1024)} %param.8) | copy-start | bytes 12292
  14.6 4.0 %copy-start.4 = (bf16[1,1024,512]{2,1,0:T(8,128)(2,1)}, bf16[1,1024,512]{2,1,0:T(8,128)(2,1)S(1)}, u32[]{:S(2)}) copy-start(bf16[1,1024,512]{2,1,0:T(8,128)(2,1)S(1)} %fusion.34) | copy-start | bytes 3145732
  18.6 1.8 copy-start.1
  18.6 7.5 %copy-start.24 = (s32[8]{0:T(128)S(1)}, s32[8]{0:T(128)}, u32[]{:S(2)}) copy-start(s32[8]{0:T(128)} %param.13) | copy-start | bytes 100
  20.4 13.0 %collective-permute-start.1 = (bf16[4,64,512]{2,1,0:T(8,128)(2,1)}, bf16[4,64,512]{2,1,0:T(8,128)(2,1)S(1)}, u32[]{:S(2)}, u32[]{:S(2)}) collective-permute-start(bf16[4,64,512]{2,1,0:T(8,128)(2,1)} %get-tuple-element.29), channel_id=1, source_target_pairs={{4,0},{8,4},{12,8},{16,12},{20,16},{24,20},{28,24},{5,1},{9,5},{13... | collective-permute-start | bytes 786440 | tf_op jit(solution)/shard_map/ppermute | solution.py:19
  21.7 11.7 %collective-permute-start = (bf16[4,64,512]{2,1,0:T(8,128)(2,1)}, bf16[4,64,512]{2,1,0:T(8,128)(2,1)}, u32[]{:S(2)}, u32[]{:S(2)}) collective-permute-start(bf16[4,64,512]{2,1,0:T(8,128)(2,1)} %get-tuple-element.30), channel_id=1, source_target_pairs={{0,4},{4,8},{8,12},{12,16},{16,20},{20,24},{24,28},{1,5},{5,9},{9,... | collective-permute-start | bytes 786440 | tf_op jit(solution)/shard_map/ppermute | solution.py:16
  65.6 1.6 copy-start.14
  65.6 1.9 copy-start.13
  68.9 3.2 %copy-start.7 = (bf16[34,96,4,128]{3,1,2,0:T(8,128)(2,1)}, bf16[34,96,4,128]{3,1,2,0:T(8,128)(2,1)S(1)}, u32[]{:S(2)}) copy-start(bf16[34,96,4,128]{3,1,2,0:T(8,128)(2,1)S(1)} %copy_dynamic-update-slice_fusion) | copy-start | bytes 10027012
  69.0 3.2 %copy-start.11 = (bf16[34,32,4,128]{3,2,1,0:T(4,128)(2,1)S(1)}, bf16[34,32,4,128]{3,2,1,0:T(4,128)(2,1)}, u32[]{:S(2)}) copy-start(bf16[34,32,4,128]{3,2,1,0:T(4,128)(2,1)} %slice.194) | copy-start | bytes 3342340
  73.8 1.8 copy-start.6
  75.6 2.2 copy-start.5
  175.2 2.4 copy-start.15
  185.5 115.5 %reduce-scatter.3.cloned.1.call-start = ((), (), s32[]{:S(2)}) async-start(), calls=%async_computation.3 | async-start | bytes 7077888 | tf_op jit(solution)/shard_map/reduce_scatter | solution.py:164
  195.0 109.2 %reduce-scatter.5.cloned.1.call-start = ((), (), s32[]{:S(2)}) async-start(), calls=%async_computation.4 | async-start | bytes 2359296 | tf_op jit(solution)/shard_map/reduce_scatter | solution.py:165
  206.4 2.0 copy-start.16
  206.4 2.0 copy-start.21
  (8 other events, 9.4 us)
Sparse Core Ops, SparseCore 0:
  185.6 109.9 all-reduce.8
Sparse Core Ops, SparseCore 1:
  195.1 71.6 reduce-scatter.2
  269.5 34.7 reduce-scatter.4
where the time goes:
time: 317 us; the launch traced here: 312 us
  matrix products  115 us (36%)
  waiting for transfers between devices  85.6 us (27%)
  local copies, waits for them, and re-layouts  64.8 us (20%)
  other arithmetic  24.9 us (8%)
  between operations  16.1 us (5%)
  starting transfers between devices  5.15 us (2%)
    psum x1, waiting for transfers between devices, on_device(): head_total = lax.psum(incoming, 'mp')  84.6 us
    dot_general x1, matrix products, attend(): jnp.einsum('chij,cihd->cjhd', score_grad, queries, preferred_element_type...  31.5 us
    dot_general x1, matrix products, attend(): jnp.einsum('chij,cjhd->cihd', score_grad, key_win, preferred_element_type...  28.3 us
    dot_general x1, matrix products, attend(): jnp.einsum('chij,cihd->cjhd', rounded, grad_rows, preferred_element_type=...  13.4 us
    unnamed x57, local copies, waits for them, and re-layouts  13.1 us
    dot_general x1, matrix products, attend(): jnp.einsum('chij,cjhd->cihd', rounded, value_win, preferred_element_type=...  11.3 us
    dot_general x1, matrix products, on_device(): jnp.einsum('rd,mrh->mdh', normed, all_grads, preferred_element_type=jnp.f...  8.83 us
    another operation x4, local copies, waits for them, and re-layouts, on_device(): jnp.stack([query_grad, key_grad, value_grad])  8 us
  transfers between devices with their start and end apart: 5, of which 2 were waited for; matrix products, arithmetic and copies ran while one was open for 12% of the time, Pallas kernels for 0%

commit v1 on v0

--- a/solution.py
+++ b/solution.py
@@ -165,7 +165,7 @@
         lax.psum_scatter(out_terms, "tm", scatter_dimension=1, tiled=True),
     )
     incoming = jnp.einsum("mrh,mdh->rd", all_grads, qkv_weight, preferred_element_type=jnp.float32)
-    head_total = lax.psum(incoming, "mp")
+    head_total = incoming + lax.ppermute(incoming, "mp", [(0, 1), (1, 0)])
     full_grad = norm_backward(head_total, normal_form, inverse, norm_gain)
     share_cols = full_grad.shape[1] // lax.axis_size("mp")
     frame_grad = lax.dynamic_slice_in_dim(

time: 317 us -> 316 us (level)
  waiting for transfers between devices: 85.6 us -> 75.8 us
  local copies, waits for them, and re-layouts: 64.8 us -> 71.9 us
    psum x1 -> x0, waiting for transfers between devices: 84.6 us -> none  [on_device(): head_total = lax.psum(incoming, 'mp')]
    ppermute x0 -> x1, waiting for transfers between devices: none -> 75.8 us  [on_device(): head_total = incoming + lax.ppermute(incoming, 'mp', [(0, 1), (1, 0)])]
    unnamed x57 -> x59, local copies, waits for them, and re-layouts: 13.1 us -> 18.8 us
  transfers between devices with their start and end apart: 5 -> 5, of which waited for: 2 -> 1; matrix products, arithmetic and copies ran while one was open for 12% -> 13% of each run, Pallas kernels for 0% -> 0%
where the time goes in v1:
time: 316 us; the launch traced here: 311 us
  matrix products  114 us (36%)
  waiting for transfers between devices  75.8 us (24%)
  local copies, waits for them, and re-layouts  71.9 us (23%)
  other arithmetic  26.1 us (8%)
  between operations  14.7 us (5%)
  starting transfers between devices  8.11 us (3%)
    ppermute x1, waiting for transfers between devices, on_device(): head_total = incoming + lax.ppermute(incoming, 'mp', [(0, 1), (1, 0)])  75.8 us
    dot_general x1, matrix products, attend(): jnp.einsum('chij,cihd->cjhd', score_grad, queries, preferred_element_type...  31.5 us
    dot_general x1, matrix products, attend(): jnp.einsum('chij,cjhd->cihd', score_grad, key_win, preferred_element_type...  28.3 us
    unnamed x59, local copies, waits for them, and re-layouts  18.8 us
    dot_general x1, matrix products, attend(): jnp.einsum('chij,cihd->cjhd', rounded, grad_rows, preferred_element_type=...  13.4 us
    dot_general x1, matrix products, attend(): jnp.einsum('chij,cjhd->cihd', rounded, value_win, preferred_element_type=...  11.3 us
    another operation x4, local copies, waits for them, and re-layouts, on_device(): jnp.stack([query_grad, key_grad, value_grad])  9.29 us
    dot_general x1, matrix products, on_device(): jnp.einsum('rd,mrh->mdh', normed, all_grads, preferred_element_type=jnp.f...  7.78 us
  transfers between devices with their start and end apart: 5, of which 1 were waited for; matrix products, arithmetic and copies ran while one was open for 13% of the time, Pallas kernels for 0%

profile of v1, /device:TPU:0, one launch (start us, length us, event | category | flops | bytes accessed | tf_op | source)
XLA Modules:
  0.0 310.7 jit_solution(18368102848599103037)
XLA Ops:
  7.2 4.1 %copy.46 = bf16[1024,1024]{0,1:T(8,128)(2,1)} copy(bf16[1024,1024]{1,0:T(8,128)(2,1)} %param.7) | data formatting | bytes 4194304 | tf_op args[0]
  14.3 3.3 %fusion.34 = bf16[1,1024,512]{2,1,0:T(8,128)(2,1)S(1)} fusion(bf16[512,1024]{1,0:T(8,128)(2,1)} %param.10, bf16[1024,1024]{1,0:T(8,128)(2,1)} %param.11, bf16[1024]{0:T(1024)(128)(2,1)S(1)} %dynamic-slice_convert_fusion), kind=kOutput, calls=%fused_computation.43 | convolution fusion | flops 1075314688 | bytes 4196352 | tf_op jit(solution)/shard_map/dot_general | solution.py:126
  17.6 3.9 %convert_bitcast_fusion = bf16[3,1024,512]{2,1,0:T(8,128)(2,1)S(1)} fusion(bf16[3,1024,512]{2,1,0:T(8,128)(2,1)S(1)} %copy-done, f32[1024]{0:T(1024)S(1)} %copy-done.22, f32[1024]{0:T(1024)S(1)} %add_rsqrt_fusion, f32[1024]{0:T(1024)S(1)} %broadcast_multiply_fusion.2, bf16[1024,1024]{0,1:T(8,128)(2,1)S(1)} %copy-done.2), kind=kOutput, calls=%fused_computation.10 | convolution fusion | flops 3228041216 | bytes 8400896 | tf_op jit(solution)/shard_map/rd,mdh->mrh/dot_general | solution.py:121
  24.6 3.8 %collective-permute-start = (bf16[4,64,512]{2,1,0:T(8,128)(2,1)}, bf16[4,64,512]{2,1,0:T(8,128)(2,1)}, u32[]{:S(2)}, u32[]{:S(2)}) collective-permute-start(bf16[4,64,512]{2,1,0:T(8,128)(2,1)} %get-tuple-element.30), channel_id=1, source_target_pairs={{0,4},{4,8},{8,12},{12,16},{16,20},{20,24},{24,28},{1,5},{5,9},{9,... | collective-permute-start | bytes 786440 | tf_op jit(solution)/shard_map/ppermute | solution.py:16
  36.4 3.2 %pad_maximum_fusion = (bf16[1,1088,512]{2,1,0:T(8,128)(2,1)}, bf16[1,1088,512]{2,1,0:T(8,128)(2,1)}, bf16[1,1088,512]{2,1,0:T(8,128)(2,1)}) fusion(bf16[4,64,512]{2,1,0:T(8,128)(2,1)S(1)} %collective-permute-done.1, bf16[1,1024,512]{2,1,0:T(8,128)(2,1)} %copy-done.5, bf16[3,1024,512]{2,1,0:T(8,128)(2,1)} %copy-done.4, ...), kind=kLoop, calls=%fused_computation.44 | loop fusion | flops 10027008 | bytes 8060928 | tf_op jit(solution)/shard_map/concatenate | solution.py:20
  39.6 3.1 slice.216
  42.7 4.3 %pad_maximum_fusion.11 = (bf16[1,1088,512]{2,1,0:T(8,128)(2,1)}, bf16[1,1088,512]{2,1,0:T(8,128)(2,1)}, bf16[1,1088,512]{2,1,0:T(8,128)(2,1)}, bf16[1,1088,512]{2,1,0:T(8,128)(2,1)}, bf16[1,1088,512]{2,1,0:T(8,128)(2,1)}) fusion(bf16[4,64,512]{2,1,0:T(8,128)(2,1)S(1)} %collective-permute-done.1, bf16[4,64,512]{2,1,0:T(8,128)(2,1)} %collective-permute-done, ...), kind=kLoop, calls=%fused_computation.55 | loop fusion | flops 21168128 | bytes 10289152 | tf_op jit(solution)/shard_map/slice | solution.py:145
  47.1 3.1 reshape_squeeze.8
  50.1 3.1 reshape_squeeze.9
  53.3 3.1 slice.194
  56.3 3.1 slice.214
  59.4 3.1 slice.191
  65.6 3.1 slice.212
  72.1 3.2 %fusion.47 = f32[34,4,32,96]{3,2,1,0:T(8,128)} fusion(bf16[34,96,4,128]{3,1,2,0:T(8,128)(2,1)S(1)} %copy_dynamic-update-slice_fusion, bf16[34,32,4,128]{3,2,1,0:T(4,128)(2,1)S(1)} %copy-done.9), kind=kOutput, calls=%fused_computation.73 | convolution fusion | flops 106954752 | bytes 6127616 | tf_op jit(solution)/shard_map/cihd,cjhd->chij/dot_general | solution.py:98
  80.9 28.3 %fusion.31 = bf16[34,32,4,128]{3,1,2,0:T(8,128)(2,1)} fusion(bf16[34,96,4,128]{3,1,2,0:T(8,128)(2,1)} %copy-done.7, f32[34,4,32,96]{3,2,1,0:T(8,128)} %fusion.47, f32[34,4,32,96]{3,2,1,0:T(8,128)} %get-tuple-element.42, f32[34,4,32]{2,1,0:T(4,128)S(1)} %get-tuple-element.41), kind=kOutput, calls=%fused_computation.42 | convolution fusion | flops 110440800 | bytes 7816192 | tf_op jit(solution)/shard_map/chij,cjhd->cihd/dot_general | solution.py:103
  109.3 31.5 %convolution_bitcast_fusion.1 = f32[34,96,4,128]{3,1,2,0:T(8,128)} fusion(f32[34,4,32,96]{3,2,1,0:T(8,128)} %fusion.47, bf16[34,32,4,128]{3,2,1,0:T(4,128)(2,1)} %reshape_squeeze.8, f32[34,4,32,96]{3,2,1,0:T(8,128)} %get-tuple-element.42, f32[34,4,32]{2,1,0:T(4,128)S(1)} %get-tuple-element.41), kind=kOutput, calls=%fused_computation.12 | convolution fusion | flops 109883744 | bytes 11158528 | tf_op jit(solution)/shard_map/chij,cihd->cjhd/dot_general | solution.py:107
  140.8 13.4 %convolution_bitcast_fusion = f32[34,96,4,128]{3,1,2,0:T(8,128)} fusion(bf16[34,32,4,128]{3,2,1,0:T(4,128)(2,1)} %reshape_squeeze.9, f32[34,4,32]{2,1,0:T(4,128)S(1)} %get-tuple-element.41, f32[34,4,32,96]{3,2,1,0:T(8,128)} %copy-done.6, pred[34,32,96]{2,1,0:T(8,128)(4,1)S(1)} %or_and_fusion), kind=kOutput, calls=%fused_computation.11 | convolution fusion | flops 109048160 | bytes 9591808 | tf_op jit(solution)/shard_map/chij,cihd->cjhd/dot_general | solution.py:110
  159.2 3.8 %fusion.64 = (f32[34,32,4,128]{3,1,2,0:T(8,128)S(1)}, f32[34,32,4,128]{3,1,2,0:T(8,128)S(1)}, f32[34,32,4,128]{3,1,2,0:T(8,128)S(1)}) fusion(f32[34,96,4,128]{3,1,2,0:T(8,128)} %convolution_bitcast_fusion.1), kind=kLoop, calls=%fused_computation.111 | loop fusion | bytes 13369344 | tf_op jit(solution)/shard_map/slice | solution.py:51
  169.8 3.8 %fusion.63 = (f32[34,32,4,128]{3,1,2,0:T(8,128)S(1)}, f32[34,32,4,128]{3,1,2,0:T(8,128)S(1)}, f32[34,32,4,128]{3,1,2,0:T(8,128)S(1)}) fusion(f32[34,96,4,128]{3,1,2,0:T(8,128)} %convolution_bitcast_fusion), kind=kLoop, calls=%fused_computation.110 | loop fusion | bytes 13369344 | tf_op jit(solution)/shard_map/slice | solution.py:51
  183.1 7.8 %convolution_bitcast_fusion.2 = f32[3,1024,512]{1,2,0:T(8,128)} fusion(bf16[3,1024,512]{2,1,0:T(8,128)(2,1)} %constant_dynamic-update-slice_fusion, f32[1024]{0:T(1024)S(1)} %copy-done.23, f32[1024]{0:T(1024)S(1)} %add_rsqrt_fusion, f32[1024]{0:T(1024)S(1)} %copy-done.19, bf16[1024,1024]{0,1:T(8,128)(2,1)S(1)} %copy-done.3), kind=kOutput, calls=%fused_computation.13 | convolution fusion | flops 3226468352 | bytes 11546624 | tf_op jit(solution)/shard_map/rd,mrh->mdh/dot_general | solution.py:161
  191.0 6.9 %convolution_bitcast_fusion.3 = f32[1024,1024]{0,1:T(8,128)} fusion(bf16[3,1024,512]{2,1,0:T(8,128)(2,1)} %constant_dynamic-update-slice_fusion, bf16[3,1024,512]{2,1,0:T(8,128)(2,1)S(1)} %copy-done), kind=kOutput, calls=%fused_computation.19 | convolution fusion | flops 3221225472 | bytes 10485760 | tf_op jit(solution)/shard_map/mrh,mdh->rd/dot_general | solution.py:167
  200.9 11.3 %fusion.30 = bf16[34,32,4,128]{3,1,2,0:T(8,128)(2,1)} fusion(bf16[34,96,4,128]{3,1,2,0:T(8,128)(2,1)} %copy-done.8, f32[34,4,32]{2,1,0:T(4,128)S(1)} %get-tuple-element.41, f32[34,4,32,96]{3,2,1,0:T(8,128)} %copy-done.6, pred[34,32,96]{2,1,0:T(8,128)(4,1)S(1)} %or_and_fusion), kind=kOutput, calls=%fused_computation.41 | convolution fusion | flops 109605216 | bytes 6249472 | tf_op jit(solution)/shard_map/chij,cjhd->cihd/dot_general | solution.py:95
  216.8 75.8 %collective-permute-done.2 = f32[1024,1024]{0,1:T(8,128)} collective-permute-done((f32[1024,1024]{0,1:T(8,128)}, f32[1024,1024]{0,1:T(8,128)}, u32[]{:S(2)}, u32[]{:S(2)}) %collective-permute-start.2) | collective-permute-done | bytes 4194336 | tf_op jit(solution)/shard_map/ppermute | solution.py:168
  292.6 5.0 %fusion.62 = (f32[1024]{0:T(1024)S(1)}, f32[1024]{0:T(1024)S(1)}, f32[1024,1024]{0,1:T(8,128)S(1)}, f32[1024,1024]{0,1:T(8,128)S(1)}) fusion(f32[1024]{0:T(1024)S(1)} %add_rsqrt_fusion, f32[1024]{0:T(1024)S(1)} %copy-done.19, bf16[1024,1024]{0,1:T(8,128)(2,1)} %copy.46, f32[1024]{0:T(1024)S(1)} %copy-done.23, f32[1024,1024]{0,1:T(8,128)} %convolution_bitcast_fusion.3, ...), kind=kLoop, calls=%fused_computation.109 | loop fusion | flops 8386560 | bytes 18894848 | tf_op jit(solution)/shard_map/reduce_sum | solution.py:34
  (117 shorter events, 61.0 us)
Async XLA Ops:
  7.2 10.4 %copy-start = (bf16[3,1024,512]{2,1,0:T(8,128)(2,1)S(1)}, bf16[3,1024,512]{2,1,0:T(8,128)(2,1)}, u32[]{:S(2)}) copy-start(bf16[3,1024,512]{2,1,0:T(8,128)(2,1)} %param.9) | copy-start | bytes 9437188
  7.2 294.2 %reduce-scatter.3.cloned.1.call-start = ((), (), s32[]{:S(2)}) async-start(), calls=%async_computation.2 | async-start | bytes 7077888 | tf_op jit(solution)/shard_map/reduce_scatter | solution.py:164
  11.4 2.2 copy-start.1
  11.4 2.8 copy-start.17
  13.6 4.0 %copy-start.18 = (f32[1024]{0:T(1024)}, f32[1024]{0:T(1024)S(1)}, u32[]{:S(2)}) copy-start(f32[1024]{0:T(1024)S(1)} %broadcast_multiply_fusion.2) | copy-start | bytes 12292
  14.2 3.4 %copy-start.20 = (bf16[1024]{0:T(1024)(128)(2,1)}, bf16[1024]{0:T(1024)(128)(2,1)S(1)}, u32[]{:S(2)}) copy-start(bf16[1024]{0:T(1024)(128)(2,1)S(1)} %dynamic-slice_convert_fusion) | copy-start | bytes 6148
  14.2 3.4 %copy-start.2 = (bf16[1024,1024]{0,1:T(8,128)(2,1)S(1)}, bf16[1024,1024]{0,1:T(8,128)(2,1)}, u32[]{:S(2)}) copy-start(bf16[1024,1024]{0,1:T(8,128)(2,1)} %copy.46) | copy-start | bytes 6291460
  14.3 3.4 %copy-start.22 = (f32[1024]{0:T(1024)S(1)}, f32[1024]{0:T(1024)}, u32[]{:S(2)}) copy-start(f32[1024]{0:T(1024)} %param.8) | copy-start | bytes 12292
  17.6 3.9 %copy-start.5 = (bf16[1,1024,512]{2,1,0:T(8,128)(2,1)}, bf16[1,1024,512]{2,1,0:T(8,128)(2,1)S(1)}, u32[]{:S(2)}) copy-start(bf16[1,1024,512]{2,1,0:T(8,128)(2,1)S(1)} %fusion.34) | copy-start | bytes 3145732
  21.6 7.5 %copy-start.24 = (s32[8]{0:T(128)S(1)}, s32[8]{0:T(128)}, u32[]{:S(2)}) copy-start(s32[8]{0:T(128)} %param.13) | copy-start | bytes 100
  23.4 13.0 %collective-permute-start.1 = (bf16[4,64,512]{2,1,0:T(8,128)(2,1)}, bf16[4,64,512]{2,1,0:T(8,128)(2,1)S(1)}, u32[]{:S(2)}, u32[]{:S(2)}) collective-permute-start(bf16[4,64,512]{2,1,0:T(8,128)(2,1)} %get-tuple-element.29), channel_id=1, source_target_pairs={{4,0},{8,4},{12,8},{16,12},{20,16},{24,20},{28,24},{5,1},{9,5},{13... | collective-permute-start | bytes 786440 | tf_op jit(solution)/shard_map/ppermute | solution.py:19
  24.6 11.8 %collective-permute-start = (bf16[4,64,512]{2,1,0:T(8,128)(2,1)}, bf16[4,64,512]{2,1,0:T(8,128)(2,1)}, u32[]{:S(2)}, u32[]{:S(2)}) collective-permute-start(bf16[4,64,512]{2,1,0:T(8,128)(2,1)} %get-tuple-element.30), channel_id=1, source_target_pairs={{0,4},{4,8},{8,12},{12,16},{16,20},{20,24},{24,28},{1,5},{5,9},{9,... | collective-permute-start | bytes 786440 | tf_op jit(solution)/shard_map/ppermute | solution.py:16
  68.7 1.9 copy-start.14
  72.1 3.2 %copy-start.8 = (bf16[34,96,4,128]{3,1,2,0:T(8,128)(2,1)}, bf16[34,96,4,128]{3,1,2,0:T(8,128)(2,1)S(1)}, u32[]{:S(2)}) copy-start(bf16[34,96,4,128]{3,1,2,0:T(8,128)(2,1)S(1)} %copy_dynamic-update-slice_fusion) | copy-start | bytes 10027012
  72.1 3.2 %copy-start.12 = (bf16[34,32,4,128]{3,2,1,0:T(4,128)(2,1)S(1)}, bf16[34,32,4,128]{3,2,1,0:T(4,128)(2,1)}, u32[]{:S(2)}) copy-start(bf16[34,32,4,128]{3,2,1,0:T(4,128)(2,1)} %slice.194) | copy-start | bytes 3342340
  76.9 1.8 copy-start.7
  78.7 2.2 copy-start.6
  178.4 4.7 %copy-start.3 = (bf16[1024,1024]{0,1:T(8,128)(2,1)S(1)}, bf16[1024,1024]{0,1:T(8,128)(2,1)}, u32[]{:S(2)}) copy-start(bf16[1024,1024]{0,1:T(8,128)(2,1)} %copy.46) | copy-start | bytes 6291460
  178.4 4.7 %copy-start.19 = (f32[1024]{0:T(1024)S(1)}, f32[1024]{0:T(1024)}, u32[]{:S(2)}) copy-start(f32[1024]{0:T(1024)} %copy-done.18) | copy-start | bytes 12292
  178.4 4.7 %copy-start.23 = (f32[1024]{0:T(1024)S(1)}, f32[1024]{0:T(1024)}, u32[]{:S(2)}) copy-start(f32[1024]{0:T(1024)} %param.8) | copy-start | bytes 12292
  190.9 112.7 %reduce-scatter.5.cloned.1.call-start = ((), (), s32[]{:S(2)}) async-start(), calls=%async_computation.3 | async-start | bytes 2359296 | tf_op jit(solution)/shard_map/reduce_scatter | solution.py:165
  197.9 94.7 %collective-permute-start.2 = (f32[1024,1024]{0,1:T(8,128)}, f32[1024,1024]{0,1:T(8,128)}, u32[]{:S(2)}, u32[]{:S(2)}) collective-permute-start(f32[1024,1024]{0,1:T(8,128)} %convolution_bitcast_fusion.3), channel_id=1, source_target_pairs={{0,2},{2,0},{1,3},{3,1},{4,6},{6,4},{5,7},{7,5},{8,10},{10,8},{9,1... | collective-permute-start | bytes 12582920 | tf_op jit(solution)/shard_map/ppermute | solution.py:168
  212.2 1.9 copy-start.16
  212.2 1.9 copy-start.21
  (8 other events, 11.5 us)
Sparse Core Ops, SparseCore 0:
  191.0 71.7 reduce-scatter.2
  265.7 34.4 reduce-scatter.4
